TPU v7x, 32 devices: a whole 2x2x4 slice. The times are simulated.
32 devices in a mesh: groups: 2 (over x), node: 8 (over z, y), rep: 2 (over core).
Axes of the slice: x: 2, y: 2, z: 4, core: 2. Of those that a mesh axis runs over, the one named last changes fastest.
Arguments:
- normed_input: bfloat16 [4, 1024, 5120], P(('groups', 'rep'), 'node'), parts along dimension 0, may hold values from -6 to 6
- queries: bfloat16 [4, 1024, 2560], P(('groups', 'rep'), 'node'), parts along dimension 0, may hold values from -120 to 120
- rotated_key_heads: bfloat16 [4, 1024, 512], P(('groups', 'rep'), 'node'), parts along dimension 0, may hold values from -6 to 6
- frozen_value_rows: bfloat16 [4, 1024, 512], P(('groups', 'rep'), 'node'), parts along dimension 0, may hold values from -6 to 6
- adapter_down_weight: bfloat16 [5120, 32], replicated, may hold values from -0.078125 to 0.078125
- adapter_up_weight: bfloat16 [32, 512], replicated, may hold values from -1 to 1
- output_gradient: bfloat16 [4, 1024, 2560], P(('groups', 'rep'), 'node'), parts along dimension 0, may hold values from -6 to 6
- parents: int32 [4, 8], P(('groups', 'rep')), parts along dimension 0, may hold values from -1 to 6, as said below
- lengths: int32 [4, 8], P(('groups', 'rep')), parts along dimension 0, may hold values from 32 to 128, as said below
Outputs:
- attended: bfloat16 [4, 1024, 2560], P(('groups', 'rep'), 'node'), parts along dimension 0
- query_grad: bfloat16 [4, 1024, 2560], P(('groups', 'rep'), 'node'), parts along dimension 0
- down_grad: float32 [10240, 32], P('groups'), parts along dimension 0
- up_grad: float32 [64, 512], P('groups'), parts along dimension 0
There are 2 independent parts, one for each index of `groups`. A program takes and returns all parts, laid end to end along the dimension named above; an argument that names none is the same for every part. Nothing has to cross between parts.
Inputs may be any that keep to these rules, and one draw needn't show every extreme that they name: `parents`: slots 0 to 1 form the shared prompt, each the parent of the next, slot 0 the root. Every other slot's parent is slot 1 or a slot below it, and every ancestor of a slot s outside the prompt lies among the slots s - 5 to s - 1. `lengths`: prompt blocks are full.
All inputs are finite; a program needn't handle non-finite values.
Results may differ from a plain program's by a relative error of at most 0.0062.
Values may be sent and summed in bfloat16 or wider, within the bound.
A program may use at most 128 MiB of HBM per device.

v0:
```python
import functools
import math

import jax
import jax.numpy as jnp
from jax import lax
from jax.experimental import pallas as pl
from jax.experimental.pallas import tpu as pltpu
from jax.sharding import PartitionSpec as P

KEY_HEADS = 4
HEAD_SIZE = 128
PROMPT = 2
SPAN = 5
STEPS = 1 + PROMPT + SPAN
NEGATIVE = -1e30
F32 = jnp.float32
BF16 = jnp.bfloat16
NT = (((1,), (1,)), ((), ()))
NN = (((1,), (0,)), ((), ()))
TN = (((0,), (0,)), ((), ()))


def dot(a, b, dims):
    return lax.dot_general(a, b, dims, preferred_element_type=F32)


def attention_kernel(
    parents, lengths, q_ref, g_ref, k_ref, v_ref, low_ref, up_ref,
    att_ref, qg_ref, proj_ref, upg_ref,
    cand, score, out_acc, qg_acc, grad,
):
    own = lax.axis_index("node")
    head = pl.program_id(0)
    slots, block, _ = k_ref.shape
    per = q_ref.shape[1] // HEAD_SIZE
    rows = per * block
    scale = HEAD_SIZE ** -0.5

    cand[0] = own
    current = own
    count = jnp.int32(1)
    for step in range(1, STEPS):
        parent = parents[0, jnp.maximum(current, 0)]
        current = jnp.where(current >= 0, parent, -1)
        cand[step] = jnp.maximum(current, 0)
        count = count + (current >= 0).astype(jnp.int32)
    own_length = lengths[0, own]

    def stack(ref):
        return jnp.concatenate(
            [ref[:, c * HEAD_SIZE:(c + 1) * HEAD_SIZE] for c in range(per)], axis=0
        )

    live = lax.broadcasted_iota(jnp.int32, (block, HEAD_SIZE), 0) < own_length
    for c in range(per):
        part = g_ref[:, c * HEAD_SIZE:(c + 1) * HEAD_SIZE].astype(F32)
        grad[pl.ds(c * block, block), :] = jnp.where(live, part, 0.0).astype(BF16)
    query = stack(q_ref)

    column = lax.broadcasted_iota(jnp.int32, (block, block), 1)
    row = lax.broadcasted_iota(jnp.int32, (block, block), 0)

    s = dot(query, k_ref[own], NT) * (scale * math.log2(math.e))
    allowed = (column <= row) & (column < own_length)
    bias = jnp.where(allowed, 0.0, NEGATIVE)
    bias = jnp.concatenate([bias] * per, axis=0)
    s = jnp.where(bias < 0.0, NEGATIVE, s)
    score[0] = s

    def logits_step(h, top):
        slot = cand[h]
        s = dot(query, k_ref[slot], NT) * (scale * math.log2(math.e))
        col = lax.broadcasted_iota(jnp.int32, (rows, block), 1)
        s = jnp.where(col < lengths[0, slot], s, NEGATIVE)
        score[h] = s
        return jnp.maximum(top, s)

    top = lax.fori_loop(1, count, logits_step, s)
    top = jnp.max(top, axis=1, keepdims=True)

    def exp_step(h, total):
        e = jnp.exp2(score[h] - top)
        score[h] = e
        return total + e

    total = lax.fori_loop(0, count, exp_step, jnp.zeros((rows, block), F32))
    inverse = 1.0 / jnp.sum(total, axis=1, keepdims=True)

    out_acc[...] = jnp.zeros_like(out_acc)

    def output_step(h, carry):
        w = score[h] * inverse
        score[h] = w
        out_acc[...] += dot(w.astype(BF16), v_ref[cand[h]], NN)
        return carry

    lax.fori_loop(0, count, output_step, 0)

    dots = jnp.sum(grad[...].astype(F32) * out_acc[...], axis=1, keepdims=True)
    for c in range(per):
        part = out_acc[pl.ds(c * block, block), :]
        att_ref[:, c * HEAD_SIZE:(c + 1) * HEAD_SIZE] = jnp.where(live, part, 0.0).astype(BF16)

    @pl.when(head == 0)
    def _():
        proj_ref[...] = jnp.zeros_like(proj_ref)

    qg_acc[...] = jnp.zeros_like(qg_acc)
    upg_ref[...] = jnp.zeros_like(upg_ref)

    def backward_step(h, carry):
        slot = cand[h]
        g = grad[...]
        w = score[h]
        pressure = dot(g, v_ref[slot], NT)
        slopes = (w * (pressure - dots) * scale).astype(BF16)
        qg_acc[...] += dot(slopes, k_ref[slot], NN)
        value_grad = dot(w.astype(BF16), g, TN)
        high = value_grad.astype(BF16)
        lowp = (value_grad - high.astype(F32)).astype(BF16)
        proj_ref[slot] += dot(up_ref[...], high, NT) + dot(up_ref[...], lowp, NT)
        upg_ref[...] += dot(low_ref[slot], high, NN) + dot(low_ref[slot], lowp, NN)
        return carry

    lax.fori_loop(0, count, backward_step, 0)
    for c in range(per):
        qg_ref[:, c * HEAD_SIZE:(c + 1) * HEAD_SIZE] = qg_acc[pl.ds(c * block, block), :].astype(BF16)


def attention(parents, lengths, q, g, k_all, v_all, low_all, up):
    slots, block, width = k_all.shape
    heads = width // HEAD_SIZE
    rank = up.shape[0]
    group = q.shape[1] // heads
    rows = group // HEAD_SIZE * block
    smem = pl.BlockSpec(memory_space=pltpu.SMEM)
    return pl.pallas_call(
        attention_kernel,
        grid=(heads,),
        in_specs=[
            smem, smem,
            pl.BlockSpec((block, group), lambda k: (0, k)),
            pl.BlockSpec((block, group), lambda k: (0, k)),
            pl.BlockSpec((slots, block, HEAD_SIZE), lambda k: (0, 0, k)),
            pl.BlockSpec((slots, block, HEAD_SIZE), lambda k: (0, 0, k)),
            pl.BlockSpec((slots, rank, block), lambda k: (0, 0, 0)),
            pl.BlockSpec((rank, HEAD_SIZE), lambda k: (0, k)),
        ],
        out_specs=[
            pl.BlockSpec((block, group), lambda k: (0, k)),
            pl.BlockSpec((block, group), lambda k: (0, k)),
            pl.BlockSpec((slots, rank, block), lambda k: (0, 0, 0)),
            pl.BlockSpec((rank, HEAD_SIZE), lambda k: (0, k)),
        ],
        out_shape=[
            jax.ShapeDtypeStruct(q.shape, BF16),
            jax.ShapeDtypeStruct(q.shape, BF16),
            jax.ShapeDtypeStruct((slots, rank, block), F32),
            jax.ShapeDtypeStruct((rank, width), F32),
        ],
        scratch_shapes=[
            pltpu.SMEM((STEPS,), jnp.int32),
            pltpu.VMEM((STEPS, rows, block), F32),
            pltpu.VMEM((rows, HEAD_SIZE), F32),
            pltpu.VMEM((rows, HEAD_SIZE), F32),
            pltpu.VMEM((rows, HEAD_SIZE), BF16),
        ],
        compiler_params=pltpu.CompilerParams(
            dimension_semantics=("arbitrary",), vmem_limit_bytes=48 * 1024 * 1024
        ),
        name="tree_attention",
    )(parents, lengths, q, g, k_all, v_all, low_all, up)


def on_device(x, q, k, frozen, down, up, g, parents, lengths):
    x, q, k, frozen, g = x[0], q[0], k[0], frozen[0], g[0]
    block = x.shape[0]
    slots = lax.axis_size("node")
    low_t = lax.dot_general(
        down, x, (((0,), (1,)), ((), ())), preferred_element_type=F32
    ).astype(BF16)
    values = (frozen.astype(F32) + dot(low_t, up, TN)).astype(BF16)
    k_all = lax.all_gather(k, "node", axis=0)
    v_all = lax.all_gather(values, "node", axis=0)
    low_all = lax.all_gather(low_t, "node", axis=0)
    attended, query_grad, proj, up_sum = attention(
        parents, lengths, q, g, k_all, v_all, low_all, up
    )
    total = lax.psum_scatter(proj, "node", scatter_dimension=0, tiled=True)[0].astype(BF16)
    down_part = dot(total, x, NN)
    down_sum, up_total = lax.psum((down_part, up_sum), ("node", "rep"))
    factor = (slots * lax.axis_size("rep") * block) ** -0.5
    return attended[None], query_grad[None], (down_sum * factor).T, up_total * factor


def solution(mesh):
    rows = P(("groups", "rep"), "node", None)
    table = P(("groups", "rep"), None)
    return jax.shard_map(
        on_device,
        mesh=mesh,
        in_specs=(rows, rows, rows, rows, P(), P(), rows, table, table),
        out_specs=(rows, rows, P("groups", None), P("groups", None)),
        check_vma=False,
    )
```

profile of v0, /device:TPU:0, one launch (start us, length us, event | category | flops | bytes accessed | tf_op | source)
XLA Modules:
  0.0 297.5 jit_solution(655567162819351596)
XLA Ops:
  7.2 0.0 copy-start
  7.2 0.0 all-gather.5.cloned.1.call-start
  7.3 0.7 all-gather.5.cloned.1.call-update
  8.0 0.0 all-gather.7.cloned.1.call-start
  8.0 0.5 copy-done
  8.5 1.5 fusion.5
  10.0 0.0 copy-done.5
  10.0 0.9 fusion.4
  10.9 0.0 all-gather.7.cloned.1.call-update
  10.9 0.0 reduce-scatter.2.cloned.1.call-start
  11.0 32.4 %all-gather.1 = bf16[256,128]{1,0:T(8,128)(2,1)S(1)} all-gather(bf16[32,128]{1,0:T(8,128)(2,1)S(1)} %fusion.5), channel_id=3, replica_groups=mesh['groups'=2,'node'=8,'rep'=2] {'node'}, dimensions={0}, use_global_device_ids=true | all-gather | bytes 73728 | tf_op jit(solution)/shard_map/all_gather | solution.py:186
  43.4 9.9 %all-gather.5.cloned.1.call-done.k_ref = bf16[8,128,512]{2,1,0:T(8,128)(2,1)} async-done(((bf16[1,128,512]{2,1,0:T(8,128)(2,1)}), bf16[8,128,512]{2,1,0:T(8,128)(2,1)}) %all-gather.5.cloned.1.call-update) | async-done | bytes 1048592 | tf_op jit(solution)/shard_map/all_gather | solution.py:184
  53.3 41.8 %all-gather.7.cloned.1.call-done = bf16[1024,512]{1,0:T(8,128)(2,1)} async-done(((bf16[128,512]{1,0:T(8,128)(2,1)}), bf16[1024,512]{1,0:T(8,128)(2,1)}) %all-gather.7.cloned.1.call-update) | async-done | bytes 1048592 | tf_op jit(solution)/shard_map/all_gather | solution.py:185
  95.1 1.2 copy-done.1
  96.3 1.2 copy-done.2
  97.5 8.2 %tree_attention.1 = (bf16[128,2560]{1,0:T(8,128)(2,1)}, bf16[128,2560]{1,0:T(8,128)(2,1)}, f32[8,32,128]{2,1,0:T(8,128)}, f32[32,512]{1,0:T(8,128)}) custom-call(s32[1,8]{1,0:T(1,128)S(1)} %copy-done.6, s32[1,8]{1,0:T(1,128)S(1)} %copy-done.7, bf16[128,2560]{1,0:T(8,128)(2,1)S(1)} %bitcast.25, bf16[128,2560]{1,0:T(8,128)(2,1)S(1)} %bitcast.26, ...), custom_call_target="tpu_custom_call" | custom-call | tf_op jit(solution)/shard_map/tree_attention/pallas_call | solution.py:138
  105.7 0.0 reduce-scatter.2.cloned.1.call-update
  105.7 0.0 all-reduce.3.cloned.1.call-start
  105.8 88.1 %reduce-scatter.2.cloned.1.call-done = f32[1,32,128]{2,1,0:T(8,128)} async-done(((f32[8,32,128]{2,1,0:T(8,128)}), f32[1,32,128]{2,1,0:T(8,128)}) %reduce-scatter.2.cloned.1.call-update) | async-done | bytes 16400 | tf_op jit(solution)/shard_map/reduce_scatter | solution.py:190
  193.8 1.9 fusion
  195.7 0.0 all-reduce.3.cloned.1.call-update
  195.7 92.6 %all-reduce.3.cloned.1.call-done = (f32[32,5120]{1,0:T(8,128)}, f32[32,512]{1,0:T(8,128)}) async-done(((f32[32,5120]{1,0:T(8,128)}, f32[32,512]{1,0:T(8,128)}), (f32[32,5120]{1,0:T(8,128)}, f32[32,512]{1,0:T(8,128)})) %all-reduce.3.cloned.1.call-update) | async-done | bytes 720912 | tf_op jit(solution)/shard_map/psum | solution.py:192
  288.3 2.0 multiply_bitcast_fusion
  290.3 0.6 broadcast_multiply_fusion
  (15 shorter events, 0.0 us)
Async XLA Ops:
  7.2 1.3 copy-start
  7.2 2.8 copy-start.5
  7.2 2.8 copy-start.8
  7.2 87.8 %copy-start.7 = (s32[1,8]{1,0:T(1,128)S(1)}, s32[1,8]{1,0:T(1,128)}, u32[]{:S(2)}) copy-start(s32[1,8]{1,0:T(1,128)} %lengths.1) | copy-start | bytes 100
  7.2 87.8 %copy-start.6 = (s32[1,8]{1,0:T(1,128)S(1)}, s32[1,8]{1,0:T(1,128)}, u32[]{:S(2)}) copy-start(s32[1,8]{1,0:T(1,128)} %parents.1) | copy-start | bytes 100
  7.2 87.8 %copy-start.4 = (bf16[1,128,2560]{2,1,0:T(8,128)(2,1)S(1)}, bf16[1,128,2560]{2,1,0:T(8,128)(2,1)}, u32[]{:S(2)}) copy-start(bf16[1,128,2560]{2,1,0:T(8,128)(2,1)} %param.15) | copy-start | bytes 1966084
  7.2 87.8 %copy-start.3 = (bf16[1,128,2560]{2,1,0:T(8,128)(2,1)S(1)}, bf16[1,128,2560]{2,1,0:T(8,128)(2,1)}, u32[]{:S(2)}) copy-start(bf16[1,128,2560]{2,1,0:T(8,128)(2,1)} %param.10) | copy-start | bytes 1966084
  7.2 46.1 %all-gather.5.cloned.1.call-start = ((), (), s32[]{:S(2)}) async-start(), calls=%async_computation.1 | async-start | bytes 1179648 | tf_op jit(solution)/shard_map/all_gather | solution.py:184
  8.0 87.1 %all-gather.7.cloned.1.call-start = ((), (), s32[]{:S(2)}) async-start(), calls=%async_computation.3 | async-start | bytes 1179648 | tf_op jit(solution)/shard_map/all_gather | solution.py:185
  10.9 182.9 %reduce-scatter.2.cloned.1.call-start = ((), (), s32[]{:S(2)}) async-start(), calls=%async_computation.2 | async-start | bytes 147456 | tf_op jit(solution)/shard_map/reduce_scatter | solution.py:190
  95.1 1.2 copy-start.1
  96.3 1.2 copy-start.2
  105.7 182.5 %all-reduce.3.cloned.1.call-start = ((), (), s32[]{:S(2)}) async-start(), calls=%async_computation.4 | async-start | bytes 1441792 | tf_op jit(solution)/shard_map/psum | solution.py:192
  288.3 2.0 copy-start.9
Sparse Core Ops, SparseCore 0:
  10.2 43.0 all-gather.4
  56.0 39.0 all-gather.6
  105.8 87.9 reduce-scatter.1
  197.8 90.4 all-reduce.2
where the time goes:
time: 293 us; the launch traced here: 297 us
  waiting for transfers between devices  233 us (80%)
  blocking collectives  32.4 us (11%)
  between operations  13.9 us (5%)
  Pallas kernels  8.18 us (3%)
  matrix products  4.23 us (1%)
  local copies, waits for them, and re-layouts  2.96 us (1%)
    psum x1, waiting for transfers between devices, on_device(): down_sum, up_total = lax.psum((down_part, up_sum), ('node', 'rep'))  92.6 us
    reduce_scatter x1, waiting for transfers between devices, on_device(): lax.psum_scatter(proj, 'node', scatter_dimension=0, tiled=True)[0]  88.1 us
    all_gather x1, waiting for transfers between devices, on_device(): v_all = lax.all_gather(values, 'node', axis=0)  41.8 us
    all_gather x1, blocking collectives, on_device(): low_all = lax.all_gather(low_t, 'node', axis=0)  32.4 us
    all_gather x1, waiting for transfers between devices, on_device(): k_all = lax.all_gather(k, 'node', axis=0)  9.92 us
    pallas_call x1, Pallas kernels, attention(): pl.pallas_call(attention_kernel, grid=(heads,), in_specs=[smem, smem, pl....  8.18 us
  transfers between devices with their start and end apart: 4, of which 4 were waited for; matrix products, arithmetic and copies ran while one was open for 1% of the time, Pallas kernels for 0%

commit v1 on v0

--- a/solution.py
+++ b/solution.py
@@ -26,7 +26,7 @@
 
 
 def attention_kernel(
-    parents, lengths, q_ref, g_ref, k_ref, v_ref, low_ref, up_ref,
+    parents, lengths, q_ref, g_ref, own_k, own_v, own_low, k_ref, v_ref, low_ref, up_ref,
     att_ref, qg_ref, proj_ref, upg_ref,
     cand, score, out_acc, qg_acc, grad,
 ):
@@ -61,7 +61,7 @@
     column = lax.broadcasted_iota(jnp.int32, (block, block), 1)
     row = lax.broadcasted_iota(jnp.int32, (block, block), 0)
 
-    s = dot(query, k_ref[own], NT) * (scale * math.log2(math.e))
+    s = dot(query, own_k[...], NT) * (scale * math.log2(math.e))
     allowed = (column <= row) & (column < own_length)
     bias = jnp.where(allowed, 0.0, NEGATIVE)
     bias = jnp.concatenate([bias] * per, axis=0)
@@ -87,7 +87,9 @@
     total = lax.fori_loop(0, count, exp_step, jnp.zeros((rows, block), F32))
     inverse = 1.0 / jnp.sum(total, axis=1, keepdims=True)
 
-    out_acc[...] = jnp.zeros_like(out_acc)
+    w = score[0] * inverse
+    score[0] = w
+    out_acc[...] = dot(w.astype(BF16), own_v[...], NN)
 
     def output_step(h, carry):
         w = score[h] * inverse
@@ -95,7 +97,7 @@
         out_acc[...] += dot(w.astype(BF16), v_ref[cand[h]], NN)
         return carry
 
-    lax.fori_loop(0, count, output_step, 0)
+    lax.fori_loop(1, count, output_step, 0)
 
     dots = jnp.sum(grad[...].astype(F32) * out_acc[...], axis=1, keepdims=True)
     for c in range(per):
@@ -106,29 +108,33 @@
     def _():
         proj_ref[...] = jnp.zeros_like(proj_ref)
 
-    qg_acc[...] = jnp.zeros_like(qg_acc)
-    upg_ref[...] = jnp.zeros_like(upg_ref)
-
-    def backward_step(h, carry):
-        slot = cand[h]
+    def backward(h, slot, key, value, low):
         g = grad[...]
         w = score[h]
-        pressure = dot(g, v_ref[slot], NT)
+        pressure = dot(g, value, NT)
         slopes = (w * (pressure - dots) * scale).astype(BF16)
-        qg_acc[...] += dot(slopes, k_ref[slot], NN)
+        query_part = dot(slopes, key, NN)
         value_grad = dot(w.astype(BF16), g, TN)
         high = value_grad.astype(BF16)
         lowp = (value_grad - high.astype(F32)).astype(BF16)
         proj_ref[slot] += dot(up_ref[...], high, NT) + dot(up_ref[...], lowp, NT)
-        upg_ref[...] += dot(low_ref[slot], high, NN) + dot(low_ref[slot], lowp, NN)
-        return carry
-
-    lax.fori_loop(0, count, backward_step, 0)
+        return query_part, dot(low, high, NN) + dot(low, lowp, NN)
+
+    qg_acc[...], upg_ref[...] = backward(0, own, own_k[...], own_v[...], own_low[...])
+
+    def backward_step(h, carry):
+        slot = cand[h]
+        query_part, up_part = backward(h, slot, k_ref[slot], v_ref[slot], low_ref[slot])
+        qg_acc[...] += query_part
+        upg_ref[...] += up_part
+        return carry
+
+    lax.fori_loop(1, count, backward_step, 0)
     for c in range(per):
         qg_ref[:, c * HEAD_SIZE:(c + 1) * HEAD_SIZE] = qg_acc[pl.ds(c * block, block), :].astype(BF16)
 
 
-def attention(parents, lengths, q, g, k_all, v_all, low_all, up):
+def attention(parents, lengths, q, g, k, v, low, k_all, v_all, low_all, up):
     slots, block, width = k_all.shape
     heads = width // HEAD_SIZE
     rank = up.shape[0]
@@ -142,6 +148,9 @@
             smem, smem,
             pl.BlockSpec((block, group), lambda k: (0, k)),
             pl.BlockSpec((block, group), lambda k: (0, k)),
+            pl.BlockSpec((block, HEAD_SIZE), lambda k: (0, k)),
+            pl.BlockSpec((block, HEAD_SIZE), lambda k: (0, k)),
+            pl.BlockSpec((rank, block), lambda k: (0, 0)),
             pl.BlockSpec((slots, block, HEAD_SIZE), lambda k: (0, 0, k)),
             pl.BlockSpec((slots, block, HEAD_SIZE), lambda k: (0, 0, k)),
             pl.BlockSpec((slots, rank, block), lambda k: (0, 0, 0)),
@@ -170,7 +179,273 @@
             dimension_semantics=("arbitrary",), vmem_limit_bytes=48 * 1024 * 1024
         ),
         name="tree_attention",
-    )(parents, lengths, q, g, k_all, v_all, low_all, up)
+    )(parents, lengths, q, g, k, v, low, k_all, v_all, low_all, up)
+
+
+def peer(node, rep=None):
+    target = {"node": node}
+    if rep is not None:
+        target["rep"] = rep
+    return target
+
+
+def greet(slots, reps):
+    own, rep = lax.axis_index("node"), lax.axis_index("rep")
+    barrier = pltpu.get_barrier_semaphore()
+    for step in range(reps):
+        other = lax.rem(rep + step, lax.axis_size("rep"))
+
+        def signal(t, carry):
+            pl.semaphore_signal(
+                barrier, inc=1, device_id=peer(lax.rem(own + t, slots), other),
+                device_id_type=pl.DeviceIdType.MESH,
+            )
+            return carry
+
+        lax.fori_loop(0 if step else 1, slots, signal, 0)
+    pl.semaphore_wait(barrier, slots * reps - 1)
+
+
+def reaches(slot, below):
+    return (below > slot) & ((slot < PROMPT) | (below - slot <= SPAN))
+
+
+def share_kernel(slots, *refs):
+    own = lax.axis_index("node")
+    sources, targets, (send_sem, recv_sem) = refs[:3], refs[3:6], refs[6:]
+    greet(slots, 1)
+
+    def copies(local, remote, target):
+        return [
+            pltpu.make_async_remote_copy(
+                src_ref=sources[i], dst_ref=targets[i].at[remote],
+                send_sem=send_sem.at[i, target], recv_sem=recv_sem.at[i, remote],
+                device_id=peer(target), device_id_type=pl.DeviceIdType.MESH,
+            )
+            for i in range(3)
+        ]
+
+    def start(t, carry):
+        @pl.when(reaches(own, t))
+        def _():
+            for c in copies(own, own, t):
+                c.start()
+        return carry
+
+    def wait_send(t, carry):
+        @pl.when(reaches(own, t))
+        def _():
+            for c in copies(own, own, t):
+                c.wait_send()
+        return carry
+
+    def wait_recv(t, carry):
+        @pl.when(reaches(t, own))
+        def _():
+            for c in copies(own, t, t):
+                c.wait_recv()
+        return carry
+
+    lax.fori_loop(0, slots, start, 0)
+    lax.fori_loop(0, slots, wait_recv, 0)
+    lax.fori_loop(0, slots, wait_send, 0)
+
+
+def share(slots, *arrays):
+    anywhere = pl.BlockSpec(memory_space=pl.ANY)
+    return pl.pallas_call(
+        functools.partial(share_kernel, slots),
+        in_specs=[anywhere] * 3,
+        out_specs=[anywhere] * 3,
+        out_shape=[jax.ShapeDtypeStruct((slots, *a.shape), a.dtype) for a in arrays],
+        scratch_shapes=[
+            pltpu.SemaphoreType.DMA((3, slots)),
+            pltpu.SemaphoreType.DMA((3, slots)),
+        ],
+        compiler_params=pltpu.CompilerParams(collective_id=0, has_side_effects=True),
+        name="share_blocks",
+    )(*arrays)
+
+
+def combine_kernel(
+    slots, reps, factor, proj, x_ref, upg_ref, down_ref, up_ref,
+    landed, total, parts, gathered, result,
+    send_p, recv_p, send_r, recv_r, send_g, recv_g,
+):
+    own, rep = lax.axis_index("node"), lax.axis_index("rep")
+    width = x_ref.shape[1]
+    up_width = upg_ref.shape[1]
+    _, chunks, half, chunk = parts.shape
+    mesh_id = pl.DeviceIdType.MESH
+    greet(slots, reps)
+
+    def scatter(source, target):
+        return pltpu.make_async_remote_copy(
+            src_ref=proj.at[target], dst_ref=landed.at[source],
+            send_sem=send_p.at[target], recv_sem=recv_p.at[source],
+            device_id=peer(target), device_id_type=mesh_id,
+        )
+
+    def scatter_start(t, carry):
+        @pl.when(reaches(t, own))
+        def _():
+            scatter(own, t).start()
+        return carry
+
+    lax.fori_loop(0, slots, scatter_start, 0)
+    total[...] = proj[own]
+
+    def scatter_add(t, carry):
+        @pl.when(reaches(own, t))
+        def _():
+            pltpu.make_async_remote_copy(
+                src_ref=proj.at[t], dst_ref=landed.at[t],
+                send_sem=send_p.at[t], recv_sem=recv_p.at[t],
+                device_id=peer(t), device_id_type=mesh_id,
+            ).wait_recv()
+            total[...] += landed[t]
+        return carry
+
+    lax.fori_loop(0, slots, scatter_add, 0)
+    projected = total[...].astype(BF16)
+    rank = projected.shape[0]
+    for j in range(chunks):
+        low, high = j * chunk, (j + 1) * chunk
+        pieces = []
+        if low < width:
+            pieces.append(dot(projected, x_ref[:, low:min(high, width)], NN))
+        if high > width and low < width + up_width:
+            pieces.append(upg_ref[:, max(low - width, 0):min(high - width, up_width)])
+        filled = sum(p.shape[1] for p in pieces)
+        if filled < chunk:
+            pieces.append(jnp.zeros((rank, chunk - filled), F32))
+        value = (pieces[0] if len(pieces) == 1 else jnp.concatenate(pieces, axis=1)).astype(BF16)
+        for r in range(reps):
+            parts[r, j] = value[r * half:(r + 1) * half]
+
+    def reduce_copy(source, node, r, from_rep):
+        return pltpu.make_async_remote_copy(
+            src_ref=parts.at[r, node], dst_ref=gathered.at[from_rep, source],
+            send_sem=send_r.at[r, node], recv_sem=recv_r.at[from_rep, source],
+            device_id=peer(node, r), device_id_type=mesh_id,
+        )
+
+    def gather_copy(node, r, owner, owner_rep):
+        return pltpu.make_async_remote_copy(
+            src_ref=result.at[owner_rep, owner], dst_ref=result.at[owner_rep, owner],
+            send_sem=send_g.at[r, node], recv_sem=recv_g.at[owner_rep, owner],
+            device_id=peer(node, r), device_id_type=mesh_id,
+        )
+
+    def others(action):
+        for step in range(reps):
+            r = lax.rem(rep + step, reps)
+
+            def body(t, carry):
+                action(lax.rem(own + t, slots), r)
+                return carry
+
+            lax.fori_loop(0 if step else 1, slots, body, 0)
+
+    def reduce_start(node, r):
+        @pl.when(node < chunks)
+        def _():
+            reduce_copy(own, node, r, rep).start()
+
+    others(reduce_start)
+
+    @pl.when(own < chunks)
+    def _():
+        gathered[rep, own] = parts[rep, own]
+
+        def reduce_wait(node, r):
+            reduce_copy(node, own, rep, r).wait_recv()
+
+        others(reduce_wait)
+
+        def add(t, acc):
+            for r in range(reps):
+                acc = acc + gathered[r, t].astype(F32)
+            return acc
+
+        acc = lax.fori_loop(0, slots, add, jnp.zeros((half, chunk), F32))
+        result[rep, own] = (acc * factor).astype(BF16)
+
+        def gather_start(node, r):
+            gather_copy(node, r, own, rep).start()
+
+        others(gather_start)
+
+    def gather_wait(node, r):
+        @pl.when(node < chunks)
+        def _():
+            gather_copy(own, rep, node, r).wait_recv()
+
+    others(gather_wait)
+    for j in range(chunks):
+        low, high = j * chunk, (j + 1) * chunk
+        for r in range(reps):
+            rows = slice(r * half, (r + 1) * half)
+            if low < width:
+                end = min(high, width)
+                down_ref[rows, low:end] = result[r, j, :, :end - low].astype(F32)
+            if high > width and low < width + up_width:
+                a, b = max(low, width), min(high, width + up_width)
+                up_ref[rows, a - width:b - width] = result[r, j, :, a - low:b - low].astype(F32)
+
+    def scatter_drain(t, carry):
+        @pl.when(reaches(t, own))
+        def _():
+            scatter(own, t).wait_send()
+        return carry
+
+    lax.fori_loop(0, slots, scatter_drain, 0)
+
+    def reduce_drain(node, r):
+        @pl.when(node < chunks)
+        def _():
+            reduce_copy(own, node, r, rep).wait_send()
+
+    others(reduce_drain)
+
+    @pl.when(own < chunks)
+    def _():
+        others(lambda node, r: gather_copy(node, r, own, rep).wait_send())
+
+
+def combine(slots, reps, factor, proj, x, upg):
+    _, rank, block = proj.shape
+    width, up_width = x.shape[1], upg.shape[1]
+    tiles = -(-(width + up_width) // 128)
+    per = -(-tiles // slots)
+    chunks = -(-tiles // per)
+    chunk = per * 128
+    half = rank // reps
+    vmem = pl.BlockSpec(memory_space=pltpu.VMEM)
+    dma = pltpu.SemaphoreType.DMA
+    return pl.pallas_call(
+        functools.partial(combine_kernel, slots, reps, factor),
+        in_specs=[vmem] * 3,
+        out_specs=[vmem] * 2,
+        out_shape=[
+            jax.ShapeDtypeStruct((rank, width), F32),
+            jax.ShapeDtypeStruct((rank, up_width), F32),
+        ],
+        scratch_shapes=[
+            pltpu.VMEM(proj.shape, F32),
+            pltpu.VMEM((rank, block), F32),
+            pltpu.VMEM((reps, chunks, half, chunk), BF16),
+            pltpu.VMEM((reps, slots, half, chunk), BF16),
+            pltpu.VMEM((reps, chunks, half, chunk), BF16),
+            dma((slots,)), dma((slots,)),
+            dma((reps, slots)), dma((reps, slots)),
+            dma((reps, slots)), dma((reps, slots)),
+        ],
+        compiler_params=pltpu.CompilerParams(
+            collective_id=1, has_side_effects=True, vmem_limit_bytes=48 * 1024 * 1024
+        ),
+        name="combine_gradients",
+    )(proj, x, upg)
 
 
 def on_device(x, q, k, frozen, down, up, g, parents, lengths):
@@ -181,17 +456,14 @@
         down, x, (((0,), (1,)), ((), ())), preferred_element_type=F32
     ).astype(BF16)
     values = (frozen.astype(F32) + dot(low_t, up, TN)).astype(BF16)
-    k_all = lax.all_gather(k, "node", axis=0)
-    v_all = lax.all_gather(values, "node", axis=0)
-    low_all = lax.all_gather(low_t, "node", axis=0)
+    k_all, v_all, low_all = share(slots, k, values, low_t)
     attended, query_grad, proj, up_sum = attention(
-        parents, lengths, q, g, k_all, v_all, low_all, up
+        parents, lengths, q, g, k, values, low_t, k_all, v_all, low_all, up
     )
-    total = lax.psum_scatter(proj, "node", scatter_dimension=0, tiled=True)[0].astype(BF16)
-    down_part = dot(total, x, NN)
-    down_sum, up_total = lax.psum((down_part, up_sum), ("node", "rep"))
-    factor = (slots * lax.axis_size("rep") * block) ** -0.5
-    return attended[None], query_grad[None], (down_sum * factor).T, up_total * factor
+    reps = lax.axis_size("rep")
+    factor = (slots * reps * block) ** -0.5
+    down_sum, up_total = combine(slots, reps, factor, proj, x, up_sum)
+    return attended[None], query_grad[None], down_sum.T, up_total
 
 
 def solution(mesh):

time: 293 us -> 126 us (0.43); the launches traced: 297 us -> 125 us
  waiting for transfers between devices: 233 us -> 0 us
  Pallas kernels: 8.18 us -> 114 us
  blocking collectives: 32.4 us -> 0 us
  between operations: 13.9 us -> 0.79 us
  local copies, waits for them, and re-layouts: 2.96 us -> 7.31 us
    pallas_call x0 -> x2, Pallas kernels: none -> 106 us  [the longest x1 64.5 us: combine(): pl.pallas_call(functools.partial(combine_kernel, slots, reps, factor), in...]
    psum x1 -> x0, waiting for transfers between devices: 92.6 us -> none  [on_device(): down_sum, up_total = lax.psum((down_part, up_sum), ('node', 'rep'))]
    reduce_scatter x1 -> x0, waiting for transfers between devices: 88.1 us -> none  [on_device(): lax.psum_scatter(proj, 'node', scatter_dimension=0, tiled=True)[0]]
    all_gather x2 -> x0, waiting for transfers between devices: 51.7 us -> none  [the longest x1 41.8 us: on_device(): v_all = lax.all_gather(values, 'node', axis=0)]
    all_gather x1 -> x0, blocking collectives: 32.4 us -> none  [on_device(): low_all = lax.all_gather(low_t, 'node', axis=0)]
    unnamed x20 -> x32, local copies, waits for them, and re-layouts: 2.96 us -> 7.31 us
  transfers between devices with their start and end apart: 4 -> 0, of which waited for: 4 -> 0; matrix products, arithmetic and copies ran while one was open for 1% -> 0% of each run, Pallas kernels for 0% -> 0%
where the time goes in v1:
time: 126 us; the launch traced here: 125 us
  Pallas kernels  114 us (90%)
  local copies, waits for them, and re-layouts  7.31 us (6%)
  matrix products  2.71 us (2%)
    pallas_call x1, Pallas kernels, combine(): pl.pallas_call(functools.partial(combine_kernel, slots, reps, factor), in...  64.5 us
    pallas_call x1, Pallas kernels, share(): pl.pallas_call(functools.partial(share_kernel, slots), in_specs=[anywhere...  41.5 us
    pallas_call x1, Pallas kernels, attention(): pl.pallas_call(attention_kernel, grid=(heads,), in_specs=[smem, smem, pl....  7.89 us
    unnamed x32, local copies, waits for them, and re-layouts  7.31 us

profile of v1, /device:TPU:0, one launch (start us, length us, event | category | flops | bytes accessed | tf_op | source)
XLA Modules:
  0.0 124.7 jit_solution(694282944915806587)
XLA Ops:
  0.6 0.0 copy-start
  0.6 0.0 copy-start.8
  0.7 0.0 copy-start.13
  0.7 0.0 copy-start.12
  0.7 0.0 copy-start.6
  0.7 0.0 copy-start.14
  0.7 0.0 copy-start.7
  0.7 0.0 copy-start.5
  0.7 0.9 copy-done
  1.6 1.8 %convolution_convert_fusion.refs_2_.own_low = bf16[32,128]{1,0:T(8,128)(2,1)S(1)} fusion(bf16[5120,32]{0,1:T(8,128)(2,1)S(1)} %copy-done, bf16[1,128,5120]{2,1,0:T(8,128)(2,1)} %param.9), kind=kOutput, calls=%fused_computation.2 | convolution fusion | flops 41947136 | bytes 1646592 | tf_op jit(solution)/shard_map/dot_general | solution.py:455
  3.5 0.0 copy-done.8
  3.5 0.0 copy-start.9
  3.5 0.9 fusion.refs_1_.own_v
  4.4 41.5 %share_blocks.1 = (bf16[8,128,512]{2,1,0:T(8,128)(2,1)}, bf16[8,128,512]{2,1,0:T(8,128)(2,1)}, bf16[8,32,128]{2,1,0:T(8,128)(2,1)}) custom-call(bf16[128,512]{1,0:T(8,128)(2,1)} %bitcast.19, bf16[128,512]{1,0:T(8,128)(2,1)} %fusion.refs_1_.own_v, bf16[32,128]{1,0:T(8,128)(2,1)} %copy-done.9), custom_call_target="tpu_custom_call" | custom-call | tf_op jit(solution)/shard_map/share_blocks/pallas_call | solution.py:256
  45.9 0.0 copy-start.2
  45.9 0.9 copy-done.2
  46.8 1.2 copy-done.3
  48.0 1.2 copy-done.4
  49.3 0.7 copy-done.10
  50.0 0.8 copy-done.11
  50.8 7.9 %tree_attention.1 = (bf16[128,2560]{1,0:T(8,128)(2,1)}, bf16[128,2560]{1,0:T(8,128)(2,1)}, f32[8,32,128]{2,1,0:T(8,128)S(1)}, f32[32,512]{1,0:T(8,128)S(1)}) custom-call(s32[1,8]{1,0:T(1,128)S(1)} %copy-done.12, s32[1,8]{1,0:T(1,128)S(1)} %copy-done.13, bf16[128,2560]{1,0:T(8,128)(2,1)S(1)} %bitcast.17, bf16[128,2560]{1,0:T(8,128)(2,1)S(1)} %bitcast.18, ...), custom_call_target="tpu_custom_call" | custom-call | tf_op jit(solution)/shard_map/tree_attention/pallas_call | solution.py:144
  58.7 64.5 %combine_gradients.1 = (f32[32,5120]{1,0:T(8,128)S(1)}, f32[32,512]{1,0:T(8,128)S(1)}) custom-call(f32[8,32,128]{2,1,0:T(8,128)S(1)} %get-tuple-element.18.proj, bf16[128,5120]{1,0:T(8,128)(2,1)S(1)} %bitcast.15, f32[32,512]{1,0:T(8,128)S(1)} %get-tuple-element.19.upg_ref), custom_call_target="tpu_custom_call" | custom-call | tf_op jit(solution)/shard_map/combine_gradients/pallas_call | solution.py:426
  123.2 0.8 copy.15
  124.1 0.6 copy.16
  (13 shorter events, 0.0 us)
Async XLA Ops:
  0.6 1.0 copy-start
  0.6 2.8 %copy-start.8 = (bf16[32,512]{1,0:T(8,128)(2,1)S(1)}, bf16[32,512]{1,0:T(8,128)(2,1)}, u32[]{:S(2)}) copy-start(bf16[32,512]{1,0:T(8,128)(2,1)} %up_ref.1) | copy-start | bytes 98308
  0.7 45.2 %copy-start.13 = (s32[1,8]{1,0:T(1,128)S(1)}, s32[1,8]{1,0:T(1,128)}, u32[]{:S(2)}) copy-start(s32[1,8]{1,0:T(1,128)} %lengths.1) | copy-start | bytes 100
  0.7 45.2 %copy-start.12 = (s32[1,8]{1,0:T(1,128)S(1)}, s32[1,8]{1,0:T(1,128)}, u32[]{:S(2)}) copy-start(s32[1,8]{1,0:T(1,128)} %parents.1) | copy-start | bytes 100
  0.7 45.2 %copy-start.6 = (bf16[1,128,2560]{2,1,0:T(8,128)(2,1)S(1)}, bf16[1,128,2560]{2,1,0:T(8,128)(2,1)}, u32[]{:S(2)}) copy-start(bf16[1,128,2560]{2,1,0:T(8,128)(2,1)} %param.15) | copy-start | bytes 1966084
  0.7 2.8 %copy-start.14 = (bf16[1,128,512]{2,1,0:T(8,128)(2,1)S(1)}, bf16[1,128,512]{2,1,0:T(8,128)(2,1)}, u32[]{:S(2)}) copy-start(bf16[1,128,512]{2,1,0:T(8,128)(2,1)} %param.12) | copy-start | bytes 393220
  0.7 45.2 %copy-start.7 = (bf16[1,128,512]{2,1,0:T(8,128)(2,1)S(1)}, bf16[1,128,512]{2,1,0:T(8,128)(2,1)}, u32[]{:S(2)}) copy-start(bf16[1,128,512]{2,1,0:T(8,128)(2,1)} %param.11) | copy-start | bytes 393220
  0.7 45.2 %copy-start.5 = (bf16[1,128,2560]{2,1,0:T(8,128)(2,1)S(1)}, bf16[1,128,2560]{2,1,0:T(8,128)(2,1)}, u32[]{:S(2)}) copy-start(bf16[1,128,2560]{2,1,0:T(8,128)(2,1)} %param.10) | copy-start | bytes 1966084
  3.5 0.9 copy-start.9
  45.9 0.9 copy-start.2
  46.8 1.2 copy-start.3
  48.0 1.2 copy-start.4
  49.3 0.7 copy-start.10
  50.0 0.8 copy-start.11
  50.8 7.9 %copy-start.1 = (bf16[1,128,5120]{2,1,0:T(8,128)(2,1)S(1)}, bf16[1,128,5120]{2,1,0:T(8,128)(2,1)}, u32[]{:S(2)}) copy-start(bf16[1,128,5120]{2,1,0:T(8,128)(2,1)} %param.9) | copy-start | bytes 3932164

commit v2 on v1

--- a/solution.py
+++ b/solution.py
@@ -213,42 +213,68 @@
 def share_kernel(slots, *refs):
     own = lax.axis_index("node")
     sources, targets, (send_sem, recv_sem) = refs[:3], refs[3:6], refs[6:]
+    pair = own // 2
+    partner = own + 1 - 2 * lax.rem(own, 2)
     greet(slots, 1)
 
-    def copies(local, remote, target):
+    def copies(refs, slot, way, target):
         return [
             pltpu.make_async_remote_copy(
-                src_ref=sources[i], dst_ref=targets[i].at[remote],
-                send_sem=send_sem.at[i, target], recv_sem=recv_sem.at[i, remote],
+                src_ref=refs[i] if refs is sources else refs[i].at[slot],
+                dst_ref=targets[i].at[slot],
+                send_sem=send_sem.at[way, i, slot], recv_sem=recv_sem.at[i, slot],
                 device_id=peer(target), device_id_type=pl.DeviceIdType.MESH,
             )
             for i in range(3)
         ]
 
-    def start(t, carry):
-        @pl.when(reaches(own, t))
-        def _():
-            for c in copies(own, own, t):
-                c.start()
+    def onward(slot):
+        return (own + 2 < slots) & reaches(slot, 2 * pair + 2)
+
+    def each_way(refs, slot, action):
+        @pl.when(onward(slot))
+        def _():
+            for c in copies(refs, slot, 0, own + 2):
+                action(c)
+
+        @pl.when(reaches(slot, partner))
+        def _():
+            for c in copies(refs, slot, 1, partner):
+                action(c)
+
+    def relayed(action):
+        def body(step, carry):
+            slot = own - 2 * step
+
+            @pl.when(reaches(slot, 2 * pair))
+            def _():
+                action(slot)
+            return carry
+
+        lax.fori_loop(1, pair + 1, body, 0)
+
+    def arrived(slot):
+        for c in copies(targets, slot, 1, partner):
+            c.wait_recv()
+
+    def forward(slot):
+        arrived(slot)
+        each_way(targets, slot, lambda c: c.start())
+
+    each_way(sources, own, lambda c: c.start())
+    relayed(forward)
+
+    def from_partner(step, carry):
+        slot = partner - 2 * step
+
+        @pl.when(reaches(slot, own))
+        def _():
+            arrived(slot)
         return carry
 
-    def wait_send(t, carry):
-        @pl.when(reaches(own, t))
-        def _():
-            for c in copies(own, own, t):
-                c.wait_send()
-        return carry
-
-    def wait_recv(t, carry):
-        @pl.when(reaches(t, own))
-        def _():
-            for c in copies(own, t, t):
-                c.wait_recv()
-        return carry
-
-    lax.fori_loop(0, slots, start, 0)
-    lax.fori_loop(0, slots, wait_recv, 0)
-    lax.fori_loop(0, slots, wait_send, 0)
+    lax.fori_loop(0, pair + 1, from_partner, 0)
+    each_way(sources, own, lambda c: c.wait_send())
+    relayed(lambda slot: each_way(targets, slot, lambda c: c.wait_send()))
 
 
 def share(slots, *arrays):
@@ -259,7 +285,7 @@
         out_specs=[anywhere] * 3,
         out_shape=[jax.ShapeDtypeStruct((slots, *a.shape), a.dtype) for a in arrays],
         scratch_shapes=[
-            pltpu.SemaphoreType.DMA((3, slots)),
+            pltpu.SemaphoreType.DMA((2, 3, slots)),
             pltpu.SemaphoreType.DMA((3, slots)),
         ],
         compiler_params=pltpu.CompilerParams(collective_id=0, has_side_effects=True),

time: 126 us -> 105 us (0.83)
  Pallas kernels: 114 us -> 93.5 us
    pallas_call x1, Pallas kernels: 41.5 us -> 12.7 us  [share(): pl.pallas_call(functools.partial(share_kernel, slots), in_specs=[anywhere...]
    pallas_call x1, Pallas kernels: 64.5 us -> 72.9 us  [combine(): pl.pallas_call(functools.partial(combine_kernel, slots, reps, factor), in...]
where the time goes in v2:
time: 105 us; the launch traced here: 104 us
  Pallas kernels  93.5 us (89%)
  local copies, waits for them, and re-layouts  7.31 us (7%)
  matrix products  2.71 us (3%)
    pallas_call x1, Pallas kernels, combine(): pl.pallas_call(functools.partial(combine_kernel, slots, reps, factor), in...  72.9 us
    pallas_call x1, Pallas kernels, share(): pl.pallas_call(functools.partial(share_kernel, slots), in_specs=[anywhere...  12.7 us
    pallas_call x1, Pallas kernels, attention(): pl.pallas_call(attention_kernel, grid=(heads,), in_specs=[smem, smem, pl....  7.89 us
    unnamed x32, local copies, waits for them, and re-layouts  7.31 us

profile of v2, /device:TPU:0, one launch (start us, length us, event | category | flops | bytes accessed | tf_op | source)
XLA Modules:
  0.0 104.3 jit_solution(4131298601303493748)
XLA Ops:
  0.6 0.0 copy-start
  0.6 0.0 copy-start.8
  0.7 0.0 copy-start.13
  0.7 0.0 copy-start.12
  0.7 0.0 copy-start.6
  0.7 0.0 copy-start.14
  0.7 0.0 copy-start.7
  0.7 0.0 copy-start.5
  0.7 0.9 copy-done
  1.6 1.8 %convolution_convert_fusion.refs_2_.own_low = bf16[32,128]{1,0:T(8,128)(2,1)S(1)} fusion(bf16[5120,32]{0,1:T(8,128)(2,1)S(1)} %copy-done, bf16[1,128,5120]{2,1,0:T(8,128)(2,1)} %param.9), kind=kOutput, calls=%fused_computation.2 | convolution fusion | flops 41947136 | bytes 1646592 | tf_op jit(solution)/shard_map/dot_general | solution.py:481
  3.5 0.0 copy-done.8
  3.5 0.0 copy-start.9
  3.5 0.9 fusion.refs_1_.own_v
  4.4 12.7 %share_blocks.1 = (bf16[8,128,512]{2,1,0:T(8,128)(2,1)}, bf16[8,128,512]{2,1,0:T(8,128)(2,1)}, bf16[8,32,128]{2,1,0:T(8,128)(2,1)}) custom-call(bf16[128,512]{1,0:T(8,128)(2,1)} %bitcast.19, bf16[128,512]{1,0:T(8,128)(2,1)} %fusion.refs_1_.own_v, bf16[32,128]{1,0:T(8,128)(2,1)} %copy-done.9), custom_call_target="tpu_custom_call" | custom-call | tf_op jit(solution)/shard_map/share_blocks/pallas_call | solution.py:282
  17.1 0.0 copy-start.2
  17.1 0.9 copy-done.2
  18.0 1.2 %copy-done.3 = bf16[8,128,512]{2,1,0:T(8,128)(2,1)S(1)} copy-done((bf16[8,128,512]{2,1,0:T(8,128)(2,1)S(1)}, bf16[8,128,512]{2,1,0:T(8,128)(2,1)}, u32[]{:S(2)}) %copy-start.3) | copy-done | bytes 1048600
  19.2 1.2 %copy-done.4 = bf16[8,128,512]{2,1,0:T(8,128)(2,1)S(1)} copy-done((bf16[8,128,512]{2,1,0:T(8,128)(2,1)S(1)}, bf16[8,128,512]{2,1,0:T(8,128)(2,1)}, u32[]{:S(2)}) %copy-start.4) | copy-done | bytes 1048600
  20.5 0.7 copy-done.10
  21.2 0.8 copy-done.11
  22.0 7.9 %tree_attention.1 = (bf16[128,2560]{1,0:T(8,128)(2,1)}, bf16[128,2560]{1,0:T(8,128)(2,1)}, f32[8,32,128]{2,1,0:T(8,128)S(1)}, f32[32,512]{1,0:T(8,128)S(1)}) custom-call(s32[1,8]{1,0:T(1,128)S(1)} %copy-done.12, s32[1,8]{1,0:T(1,128)S(1)} %copy-done.13, bf16[128,2560]{1,0:T(8,128)(2,1)S(1)} %bitcast.17, bf16[128,2560]{1,0:T(8,128)(2,1)S(1)} %bitcast.18, ...), custom_call_target="tpu_custom_call" | custom-call | tf_op jit(solution)/shard_map/tree_attention/pallas_call | solution.py:144
  29.9 72.9 %combine_gradients.1 = (f32[32,5120]{1,0:T(8,128)S(1)}, f32[32,512]{1,0:T(8,128)S(1)}) custom-call(f32[8,32,128]{2,1,0:T(8,128)S(1)} %get-tuple-element.18.proj, bf16[128,5120]{1,0:T(8,128)(2,1)S(1)} %bitcast.15, f32[32,512]{1,0:T(8,128)S(1)} %get-tuple-element.19.upg_ref), custom_call_target="tpu_custom_call" | custom-call | tf_op jit(solution)/shard_map/combine_gradients/pallas_call | solution.py:452
  102.8 0.8 copy.15
  103.7 0.6 copy.16
  (13 shorter events, 0.0 us)
Async XLA Ops:
  0.6 1.0 copy-start
  0.6 2.8 %copy-start.8 = (bf16[32,512]{1,0:T(8,128)(2,1)S(1)}, bf16[32,512]{1,0:T(8,128)(2,1)}, u32[]{:S(2)}) copy-start(bf16[32,512]{1,0:T(8,128)(2,1)} %up_ref.1) | copy-start | bytes 98308
  0.7 16.4 %copy-start.13 = (s32[1,8]{1,0:T(1,128)S(1)}, s32[1,8]{1,0:T(1,128)}, u32[]{:S(2)}) copy-start(s32[1,8]{1,0:T(1,128)} %lengths.1) | copy-start | bytes 100
  0.7 16.4 %copy-start.12 = (s32[1,8]{1,0:T(1,128)S(1)}, s32[1,8]{1,0:T(1,128)}, u32[]{:S(2)}) copy-start(s32[1,8]{1,0:T(1,128)} %parents.1) | copy-start | bytes 100
  0.7 16.4 %copy-start.6 = (bf16[1,128,2560]{2,1,0:T(8,128)(2,1)S(1)}, bf16[1,128,2560]{2,1,0:T(8,128)(2,1)}, u32[]{:S(2)}) copy-start(bf16[1,128,2560]{2,1,0:T(8,128)(2,1)} %param.15) | copy-start | bytes 1966084
  0.7 2.8 %copy-start.14 = (bf16[1,128,512]{2,1,0:T(8,128)(2,1)S(1)}, bf16[1,128,512]{2,1,0:T(8,128)(2,1)}, u32[]{:S(2)}) copy-start(bf16[1,128,512]{2,1,0:T(8,128)(2,1)} %param.12) | copy-start | bytes 393220
  0.7 16.4 %copy-start.7 = (bf16[1,128,512]{2,1,0:T(8,128)(2,1)S(1)}, bf16[1,128,512]{2,1,0:T(8,128)(2,1)}, u32[]{:S(2)}) copy-start(bf16[1,128,512]{2,1,0:T(8,128)(2,1)} %param.11) | copy-start | bytes 393220
  0.7 16.4 %copy-start.5 = (bf16[1,128,2560]{2,1,0:T(8,128)(2,1)S(1)}, bf16[1,128,2560]{2,1,0:T(8,128)(2,1)}, u32[]{:S(2)}) copy-start(bf16[1,128,2560]{2,1,0:T(8,128)(2,1)} %param.10) | copy-start | bytes 1966084
  3.5 0.9 copy-start.9
  17.1 0.9 copy-start.2
  18.0 1.2 %copy-start.3 = (bf16[8,128,512]{2,1,0:T(8,128)(2,1)S(1)}, bf16[8,128,512]{2,1,0:T(8,128)(2,1)}, u32[]{:S(2)}) copy-start(bf16[8,128,512]{2,1,0:T(8,128)(2,1)} %get-tuple-element.13.k_ref) | copy-start | bytes 3145732
  19.2 1.2 %copy-start.4 = (bf16[8,128,512]{2,1,0:T(8,128)(2,1)S(1)}, bf16[8,128,512]{2,1,0:T(8,128)(2,1)}, u32[]{:S(2)}) copy-start(bf16[8,128,512]{2,1,0:T(8,128)(2,1)} %get-tuple-element.14.v_ref) | copy-start | bytes 3145732
  20.5 0.7 copy-start.10
  21.2 0.8 copy-start.11
  22.0 7.9 %copy-start.1 = (bf16[1,128,5120]{2,1,0:T(8,128)(2,1)S(1)}, bf16[1,128,5120]{2,1,0:T(8,128)(2,1)}, u32[]{:S(2)}) copy-start(bf16[1,128,5120]{2,1,0:T(8,128)(2,1)} %param.9) | copy-start | bytes 3932164
